TPU v7x, 32 devices: a whole 2x2x4 slice. The times are simulated.
32 devices in a mesh: space: 16 (over z, x, core), mode: 2 (over y).
Axes of the slice: x: 2, y: 2, z: 4, core: 2. Of those that a mesh axis runs over, the one named last changes fastest.
Arguments:
- field: float32 [3, 16, 128, 64, 256], P(None, 'mode', 'space'), may hold values from -6 to 6
- velocity: float32 [128, 64, 256], P('space'), may hold values from 0.1 to 1
- dispersion: float32 [128, 64, 256], P('space'), may hold values from 0.05 to 0.3
- mobility: float32 [3, 8, 16], replicated, may hold values from -0.2 to 0.2
- material: int32 [128, 64, 256], P('space'), may hold values from 0 to 7
- fixed_mask: int32 [128, 64, 256], P('space'), may hold values 0 or 1
Outputs:
- advanced: float32 [3, 16, 128, 64, 256], P(None, 'mode', 'space')
All inputs are finite; a program needn't handle non-finite values. No bound on the sum of `fixed_mask` on one device may be relied on, other than what follows from the above.
Results may differ from a plain program's by a relative error of at most 0.0001.
Values sent between devices are 32-bit elements; how exact they have to be, the bound alone decides.
A program may use at most 128 MiB of HBM per device.

v0:
```python
import math
import jax
import jax.numpy as jnp
from jax import lax
from jax.sharding import PartitionSpec as P

STEPS = 2
TIME_STEP = 0.1
MOBILE_BASE = 0.7


def padded(array, sides, width):
    for axis, dim in sides:
        size, length = (lax.axis_size(axis), array.shape[dim])
        up = [(i, (i + 1) % size) for i in range(size - 1)]
        down = [(j, i) for i, j in up]
        last = lax.slice_in_dim(array, length - width, length, axis=dim)
        first = lax.slice_in_dim(array, 0, width, axis=dim)
        before = lax.ppermute(last, axis, up)
        after = lax.ppermute(first, axis, down)
        array = jnp.concatenate([before, array, after], axis=dim)
    return array


def legendre_weight(order):
    return math.comb(2 * order, order) / 4.0**order


def triple_table(terms_count):
    entries = []
    for degree_a in range(terms_count):
        slab_values = []
        for degree_b in range(terms_count):
            row_values = []
            for degree_c in range(terms_count):
                degree_sum = degree_a + degree_b + degree_c
                halfsum = degree_sum // 2
                amount = 0.0
                if (
                    degree_sum % 2 == 0
                    and halfsum >= degree_a
                    and (halfsum >= degree_b)
                    and (halfsum >= degree_c)
                ):
                    amount = (
                        legendre_weight(halfsum - degree_a)
                        * legendre_weight(halfsum - degree_b)
                        * legendre_weight(halfsum - degree_c)
                    )
                    amount = amount / legendre_weight(halfsum) / (degree_sum + 1)
                    amount = amount * math.sqrt(
                        (2 * degree_a + 1) * (2 * degree_b + 1) * (2 * degree_c + 1)
                    )
                row_values.append(amount)
            slab_values.append(row_values)
        entries.append(slab_values)
    return jnp.asarray(entries, jnp.float32)


def stencil(x_padded, y_padded, velocity, dispersion):
    middle = x_padded[:, :, 2:-2]
    left_two = x_padded[:, :, :-4]
    left_one = x_padded[:, :, 1:-3]
    right_one = x_padded[:, :, 3:-1]
    right_two = x_padded[:, :, 4:]
    lower_y = y_padded[:, :, :, :-2]
    upper_y = y_padded[:, :, :, 2:]
    z_padded = jnp.pad(middle, ((0, 0), (0, 0), (0, 0), (0, 0), (1, 1)))
    lower_z = z_padded[:, :, :, :, :-2]
    upper_z = z_padded[:, :, :, :, 2:]
    spread = (16.0 * (left_one + right_one) - (left_two + right_two) - 30.0 * middle) / 12.0
    spread = spread + (lower_y + upper_y) + (lower_z + upper_z) - 4.0 * middle
    carried = (2.0 * right_one + 3.0 * middle - 6.0 * left_one + left_two) / 6.0
    return dispersion[None, None] * spread - velocity[None, None] * carried


def class_terms(total, class_mats, piece, picks):

    def add_class(klass, running):
        matrix = lax.dynamic_index_in_dim(class_mats, klass, 1, keepdims=False)
        mixed = jnp.einsum("mij,mjxyz->mixyz", matrix, piece, precision=lax.Precision.HIGHEST)
        chosen = lax.dynamic_index_in_dim(picks, klass, 0, keepdims=False)
        return running + chosen[None, None] * mixed

    return lax.fori_loop(0, class_mats.shape[1], add_class, total)


def on_device(field, velocity, dispersion, mobility, material, fixed_mask):
    modes = mobility.shape[2]
    classes = mobility.shape[1]
    triple = triple_table(modes)
    class_mats = jnp.einsum("ijk,mck->mcij", triple, mobility, precision=lax.Precision.HIGHEST)
    mode_count = lax.axis_size("mode")
    mode_index = lax.axis_index("mode")
    rows_local = field.shape[3] // mode_count
    picks = (material[None] == jnp.arange(classes, dtype=jnp.int32)[:, None, None, None]).astype(
        jnp.float32
    )
    movable = (1 - fixed_mask).astype(jnp.float32)

    def rows_of(array, axis):
        return lax.dynamic_slice_in_dim(array, mode_index * rows_local, rows_local, axis)

    state = lax.all_to_all(field, "mode", split_axis=3, concat_axis=1, tiled=True)
    speed_here = rows_of(velocity, 1)
    spread_here = rows_of(dispersion, 1)
    picks_here = rows_of(picks, 2)
    movable_here = rows_of(movable, 1)
    for sweep_index in range(STEPS):
        x_padded = padded(state, (("space", 2),), 2)
        y_padded = padded(state, (("mode", 3),), 1)
        operated = stencil(x_padded, y_padded, speed_here, spread_here)
        coupled = class_terms(MOBILE_BASE * operated, class_mats, operated, picks_here)
        state = state + TIME_STEP * movable_here[None, None] * coupled
    state = lax.all_to_all(state, "mode", split_axis=1, concat_axis=3, tiled=True)
    return state


def solution(mesh):
    in_specs = (
        P(None, "mode", "space", None, None),
        P("space", None, None),
        P("space", None, None),
        P(),
        P("space", None, None),
        P("space", None, None),
    )
    out_specs = P(None, "mode", "space", None, None)
    return jax.shard_map(
        on_device, mesh=mesh, in_specs=in_specs, out_specs=out_specs, check_vma=False
    )
```

profile of v0, /device:TPU:10, one launch (start us, length us, event | category | flops | bytes accessed | tf_op | source)
XLA Modules:
  0.0 968.9 jit_solution(4053792120406774539)
XLA Ops:
  0.0 0.0 copy-start
  0.0 16.7 %copy.12 = f32[3,8,8,64,256]{4,2,1,0,3:T(8,128)} copy(f32[3,8,8,64,256]{4,3,2,1,0:T(8,128)} %param.11) | data formatting | bytes 25165824 | tf_op args[0]
  16.7 152.3 %all_to_all.36 = f32[3,8,8,64,256]{4,2,1,0,3:T(8,128)} all-to-all(f32[3,8,8,64,256]{4,2,1,0,3:T(8,128)} %copy.12), channel_id=1, replica_groups=mesh['space'=16,'mode'=2] {'mode'}, dimensions={3} | all-to-all | bytes 25165824 | tf_op jit(solution)/shard_map/all_to_all | solution.py:104
  169.0 16.6 %copy.13 = f32[3,2,8,8,32,256]{5,4,3,0,2,1:T(8,128)} copy(f32[3,2,8,8,32,256]{5,3,2,0,4,1:T(8,128)} %bitcast.53) | data formatting | bytes 25165824 | tf_op jit(solution)/shard_map/all_to_all | solution.py:104
  185.6 0.0 copy-start.6
  185.6 6.8 fusion.46
  192.4 1.9 collective-permute-start
  194.3 3.6 collective-permute-start.1
  198.0 0.0 copy-done.9
  198.0 0.0 copy-done.10
  198.0 1.0 convolution_bitcast_fusion
  199.1 0.0 copy-done
  199.1 0.0 copy-done.7
  199.1 0.0 copy-done.8
  199.1 0.1 dynamic-slice_multiply_fusion
  199.2 3.6 fusion.47
  202.8 3.0 collective-permute-start.2
  205.8 1.3 collective-permute-start.3
  207.1 0.3 fusion.38
  207.4 6.1 collective-permute-done.2
  213.5 5.0 collective-permute-done.3
  218.5 46.5 %collective-permute-done = f32[3,16,2,32,256]{4,3,2,0,1:T(8,128)} collective-permute-done((f32[3,16,2,32,256]{4,3,2,0,1:T(8,128)}, f32[3,16,2,32,256]{4,3,2,0,1:T(8,128)}, u32[]{:S(2)}, u32[]{:S(2)}) %collective-permute-start) | collective-permute-done | bytes 3145760 | tf_op jit(solution)/shard_map/ppermute | solution.py:19
  265.0 0.0 collective-permute-done.1
  265.0 46.0 %broadcast_multiply_fusion.1 = (f32[3,16,8,32,256]{4,3,2,0,1:T(8,128)}, f32[3,16,8,32,256]{4,3,2,0,1:T(8,128)}) fusion(f32[8,32,256]{2,1,0:T(8,128)S(1)} %get-tuple-element.247, f32[3,16,8,32,256]{4,3,2,0,1:T(8,128)} %bitcast.52, f32[3,16,8,1,256]{4,3,2,0,1:T(1,128)} %collective-permute-done.3, f32[3,16,8,1,256]{4,3,2,0,1:T(1,128)} %collective-permute-done.2, ...), kind=kLoop, calls=%fused_computation.65 | loop fusion | flops 91226112 | bytes 45350912 | tf_op jit(solution)/shard_map/mul | solution.py:113
  311.0 20.3 %copy.14 = f32[3,16,8,32,256]{4,1,3,2,0:T(8,128)} copy(f32[3,16,8,32,256]{4,3,2,0,1:T(8,128)} %get-tuple-element.237) | data formatting | bytes 25165824 | tf_op jit(solution)/shard_map/while | solution.py:85
  331.3 20.4 %copy.16 = f32[3,16,8,32,256]{4,1,3,2,0:T(8,128)} copy(f32[3,16,8,32,256]{4,3,2,0,1:T(8,128)} %get-tuple-element.238) | data formatting | bytes 25165824 | tf_op jit(solution)/shard_map/while | solution.py:85
  351.6 153.1 %while.26 = (s32[]{:T(128)}, f32[3,16,8,32,256]{4,1,3,2,0:T(8,128)}, f32[8,8,32,256]{3,2,1,0:T(8,128)S(1)}, f32[3,8,16,16]{3,2,0,1:T(8,128)S(1)}, f32[3,16,8,32,256]{4,1,3,2,0:T(8,128)}, /*index=5*/s32[]{:T(128)}) while((s32[]{:T(128)}, f32[3,16,8,32,256]{4,1,3,2,0:T(8,128)}, f32[8,8,32,256]{3,2,1,0:T(8,128)S(1)}, ...), condition=%wide.region_1.2_spmd, body=%wide.region_0.1_spmd.sunk | while | flops 610271232 | bytes 38559820 | solution.py:85
  352.0 19.1 %multiply_add_fusion.4 = f32[3,16,8,32,256]{4,1,3,2,0:T(8,128)} fusion(f32[3,16,8,32,256]{4,1,3,2,0:T(8,128)} %get-tuple-element.318, f32[8,32,256]{2,1,0:T(8,128)S(1)} %dynamic-slice_bitcast_fusion.4, f32[3,16,8,32,256]{4,1,3,2,0:T(8,128)} %get-tuple-element.327, f32[3,8,16,16]{3,2,0,1:T(8,128)S(1)} %get-tuple-element.326, s32[]{:T(128)} %get-tuple-element.317), kind=kOutput, calls=%fused_computation.clone.1 | convolution fusion | flops 610271232 | bytes 38035460 | tf_op jit(solution)/shard_map/while/body/eval_jaxpr/mij,mjxyz->mixyz/dot_general | solution.py:81
  371.1 19.1 %multiply_add_fusion.4 = f32[3,16,8,32,256]{4,1,3,2,0:T(8,128)} fusion(f32[3,16,8,32,256]{4,1,3,2,0:T(8,128)} %get-tuple-element.318, f32[8,32,256]{2,1,0:T(8,128)S(1)} %dynamic-slice_bitcast_fusion.4, f32[3,16,8,32,256]{4,1,3,2,0:T(8,128)} %get-tuple-element.327, f32[3,8,16,16]{3,2,0,1:T(8,128)S(1)} %get-tuple-element.326, s32[]{:T(128)} %get-tuple-element.317), kind=kOutput, calls=%fused_computation.clone.1 | convolution fusion | flops 610271232 | bytes 38035460 | tf_op jit(solution)/shard_map/while/body/eval_jaxpr/mij,mjxyz->mixyz/dot_general | solution.py:81
  390.2 19.1 %multiply_add_fusion.4 = f32[3,16,8,32,256]{4,1,3,2,0:T(8,128)} fusion(f32[3,16,8,32,256]{4,1,3,2,0:T(8,128)} %get-tuple-element.318, f32[8,32,256]{2,1,0:T(8,128)S(1)} %dynamic-slice_bitcast_fusion.4, f32[3,16,8,32,256]{4,1,3,2,0:T(8,128)} %get-tuple-element.327, f32[3,8,16,16]{3,2,0,1:T(8,128)S(1)} %get-tuple-element.326, s32[]{:T(128)} %get-tuple-element.317), kind=kOutput, calls=%fused_computation.clone.1 | convolution fusion | flops 610271232 | bytes 38035460 | tf_op jit(solution)/shard_map/while/body/eval_jaxpr/mij,mjxyz->mixyz/dot_general | solution.py:81
  409.3 19.1 %multiply_add_fusion.4 = f32[3,16,8,32,256]{4,1,3,2,0:T(8,128)} fusion(f32[3,16,8,32,256]{4,1,3,2,0:T(8,128)} %get-tuple-element.318, f32[8,32,256]{2,1,0:T(8,128)S(1)} %dynamic-slice_bitcast_fusion.4, f32[3,16,8,32,256]{4,1,3,2,0:T(8,128)} %get-tuple-element.327, f32[3,8,16,16]{3,2,0,1:T(8,128)S(1)} %get-tuple-element.326, s32[]{:T(128)} %get-tuple-element.317), kind=kOutput, calls=%fused_computation.clone.1 | convolution fusion | flops 610271232 | bytes 38035460 | tf_op jit(solution)/shard_map/while/body/eval_jaxpr/mij,mjxyz->mixyz/dot_general | solution.py:81
  428.4 19.1 %multiply_add_fusion.4 = f32[3,16,8,32,256]{4,1,3,2,0:T(8,128)} fusion(f32[3,16,8,32,256]{4,1,3,2,0:T(8,128)} %get-tuple-element.318, f32[8,32,256]{2,1,0:T(8,128)S(1)} %dynamic-slice_bitcast_fusion.4, f32[3,16,8,32,256]{4,1,3,2,0:T(8,128)} %get-tuple-element.327, f32[3,8,16,16]{3,2,0,1:T(8,128)S(1)} %get-tuple-element.326, s32[]{:T(128)} %get-tuple-element.317), kind=kOutput, calls=%fused_computation.clone.1 | convolution fusion | flops 610271232 | bytes 38035460 | tf_op jit(solution)/shard_map/while/body/eval_jaxpr/mij,mjxyz->mixyz/dot_general | solution.py:81
  447.5 19.1 %multiply_add_fusion.4 = f32[3,16,8,32,256]{4,1,3,2,0:T(8,128)} fusion(f32[3,16,8,32,256]{4,1,3,2,0:T(8,128)} %get-tuple-element.318, f32[8,32,256]{2,1,0:T(8,128)S(1)} %dynamic-slice_bitcast_fusion.4, f32[3,16,8,32,256]{4,1,3,2,0:T(8,128)} %get-tuple-element.327, f32[3,8,16,16]{3,2,0,1:T(8,128)S(1)} %get-tuple-element.326, s32[]{:T(128)} %get-tuple-element.317), kind=kOutput, calls=%fused_computation.clone.1 | convolution fusion | flops 610271232 | bytes 38035460 | tf_op jit(solution)/shard_map/while/body/eval_jaxpr/mij,mjxyz->mixyz/dot_general | solution.py:81
  466.6 19.1 %multiply_add_fusion.4 = f32[3,16,8,32,256]{4,1,3,2,0:T(8,128)} fusion(f32[3,16,8,32,256]{4,1,3,2,0:T(8,128)} %get-tuple-element.318, f32[8,32,256]{2,1,0:T(8,128)S(1)} %dynamic-slice_bitcast_fusion.4, f32[3,16,8,32,256]{4,1,3,2,0:T(8,128)} %get-tuple-element.327, f32[3,8,16,16]{3,2,0,1:T(8,128)S(1)} %get-tuple-element.326, s32[]{:T(128)} %get-tuple-element.317), kind=kOutput, calls=%fused_computation.clone.1 | convolution fusion | flops 610271232 | bytes 38035460 | tf_op jit(solution)/shard_map/while/body/eval_jaxpr/mij,mjxyz->mixyz/dot_general | solution.py:81
  485.7 19.1 %multiply_add_fusion.4 = f32[3,16,8,32,256]{4,1,3,2,0:T(8,128)} fusion(f32[3,16,8,32,256]{4,1,3,2,0:T(8,128)} %get-tuple-element.318, f32[8,32,256]{2,1,0:T(8,128)S(1)} %dynamic-slice_bitcast_fusion.4, f32[3,16,8,32,256]{4,1,3,2,0:T(8,128)} %get-tuple-element.327, f32[3,8,16,16]{3,2,0,1:T(8,128)S(1)} %get-tuple-element.326, s32[]{:T(128)} %get-tuple-element.317), kind=kOutput, calls=%fused_computation.clone.1 | convolution fusion | flops 610271232 | bytes 38035460 | tf_op jit(solution)/shard_map/while/body/eval_jaxpr/mij,mjxyz->mixyz/dot_general | solution.py:81
  504.8 13.4 %fusion.37 = f32[3,16,8,32,256]{4,3,2,0,1:T(8,128)S(1)} fusion(f32[3,16,8,32,256]{4,1,3,2,0:T(8,128)} %get-tuple-element.193, f32[8,32,256]{2,1,0:T(8,128)S(1)} %fusion.40, f32[3,2,8,8,32,256]{5,4,3,0,2,1:T(8,128)} %copy.13), kind=kLoop, calls=%fused_computation.63 | loop fusion | flops 6291456 | bytes 38010880 | tf_op jit(solution)/shard_map/add | solution.py:114
  518.2 0.0 copy-start.2
  518.2 1.1 fusion.44
  519.3 1.9 collective-permute-start.4
  521.3 3.6 collective-permute-start.5
  524.9 0.6 fusion.45
  525.5 2.2 collective-permute-start.6
  527.8 1.3 collective-permute-start.7
  529.1 6.0 collective-permute-done.6
  535.0 4.1 collective-permute-done.7
  539.2 52.5 %collective-permute-done.4 = f32[3,16,2,32,256]{4,3,2,0,1:T(8,128)S(1)} collective-permute-done((f32[3,16,2,32,256]{4,3,2,0,1:T(8,128)S(1)}, f32[3,16,2,32,256]{4,3,2,0,1:T(8,128)S(1)}, u32[]{:S(2)}, u32[]{:S(2)}) %collective-permute-start.4) | collective-permute-done | bytes 3145760 | tf_op jit(solution)/shard_map/ppermute | solution.py:19
  591.6 1.7 copy-done.3
  593.4 0.0 collective-permute-done.5
  593.4 45.7 %broadcast_multiply_fusion = (f32[3,16,8,32,256]{4,3,2,0,1:T(8,128)}, f32[3,16,8,32,256]{4,3,2,0,1:T(8,128)}) fusion(f32[8,32,256]{2,1,0:T(8,128)S(1)} %get-tuple-element.247, f32[3,16,8,32,256]{4,3,2,0,1:T(8,128)} %copy-done.2, f32[3,16,8,1,256]{4,3,2,0,1:T(1,128)} %copy-done.5, f32[3,16,8,1,256]{4,3,2,0,1:T(1,128)} %copy-done.4, ...), kind=kLoop, calls=%fused_computation.64 | loop fusion | flops 91226112 | bytes 45350912 | tf_op jit(solution)/shard_map/mul | solution.py:113
  639.1 20.3 %copy.18 = f32[3,16,8,32,256]{4,1,3,2,0:T(8,128)} copy(f32[3,16,8,32,256]{4,3,2,0,1:T(8,128)} %get-tuple-element.235) | data formatting | bytes 25165824 | tf_op jit(solution)/shard_map/while | solution.py:85
  659.4 20.4 %copy.20 = f32[3,16,8,32,256]{4,1,3,2,0:T(8,128)} copy(f32[3,16,8,32,256]{4,3,2,0,1:T(8,128)} %get-tuple-element.236) | data formatting | bytes 25165824 | tf_op jit(solution)/shard_map/while | solution.py:85
  679.8 153.0 %while.27 = (s32[]{:T(128)}, f32[3,16,8,32,256]{4,1,3,2,0:T(8,128)}, f32[8,8,32,256]{3,2,1,0:T(8,128)S(1)}, f32[3,8,16,16]{3,2,0,1:T(8,128)S(1)}, f32[3,16,8,32,256]{4,1,3,2,0:T(8,128)}, /*index=5*/s32[]{:T(128)}) while((s32[]{:T(128)}, f32[3,16,8,32,256]{4,1,3,2,0:T(8,128)}, f32[8,8,32,256]{3,2,1,0:T(8,128)S(1)}, ...), condition=%wide.region_3.4_spmd, body=%wide.region_2.3_spmd.sunk | while | flops 610271232 | bytes 38559820 | solution.py:85
  680.1 19.1 %multiply_add_fusion.5 = f32[3,16,8,32,256]{4,1,3,2,0:T(8,128)} fusion(f32[3,16,8,32,256]{4,1,3,2,0:T(8,128)} %get-tuple-element.336, f32[8,32,256]{2,1,0:T(8,128)S(1)} %dynamic-slice_bitcast_fusion.5, f32[3,16,8,32,256]{4,1,3,2,0:T(8,128)} %get-tuple-element.345, f32[3,8,16,16]{3,2,0,1:T(8,128)S(1)} %get-tuple-element.344, s32[]{:T(128)} %get-tuple-element.335), kind=kOutput, calls=%fused_computation.5.clone.1 | convolution fusion | flops 610271232 | bytes 38035460 | tf_op jit(solution)/shard_map/while/body/eval_jaxpr/mij,mjxyz->mixyz/dot_general | solution.py:81
  699.2 19.1 %multiply_add_fusion.5 = f32[3,16,8,32,256]{4,1,3,2,0:T(8,128)} fusion(f32[3,16,8,32,256]{4,1,3,2,0:T(8,128)} %get-tuple-element.336, f32[8,32,256]{2,1,0:T(8,128)S(1)} %dynamic-slice_bitcast_fusion.5, f32[3,16,8,32,256]{4,1,3,2,0:T(8,128)} %get-tuple-element.345, f32[3,8,16,16]{3,2,0,1:T(8,128)S(1)} %get-tuple-element.344, s32[]{:T(128)} %get-tuple-element.335), kind=kOutput, calls=%fused_computation.5.clone.1 | convolution fusion | flops 610271232 | bytes 38035460 | tf_op jit(solution)/shard_map/while/body/eval_jaxpr/mij,mjxyz->mixyz/dot_general | solution.py:81
  718.2 19.1 %multiply_add_fusion.5 = f32[3,16,8,32,256]{4,1,3,2,0:T(8,128)} fusion(f32[3,16,8,32,256]{4,1,3,2,0:T(8,128)} %get-tuple-element.336, f32[8,32,256]{2,1,0:T(8,128)S(1)} %dynamic-slice_bitcast_fusion.5, f32[3,16,8,32,256]{4,1,3,2,0:T(8,128)} %get-tuple-element.345, f32[3,8,16,16]{3,2,0,1:T(8,128)S(1)} %get-tuple-element.344, s32[]{:T(128)} %get-tuple-element.335), kind=kOutput, calls=%fused_computation.5.clone.1 | convolution fusion | flops 610271232 | bytes 38035460 | tf_op jit(solution)/shard_map/while/body/eval_jaxpr/mij,mjxyz->mixyz/dot_general | solution.py:81
  737.3 19.1 %multiply_add_fusion.5 = f32[3,16,8,32,256]{4,1,3,2,0:T(8,128)} fusion(f32[3,16,8,32,256]{4,1,3,2,0:T(8,128)} %get-tuple-element.336, f32[8,32,256]{2,1,0:T(8,128)S(1)} %dynamic-slice_bitcast_fusion.5, f32[3,16,8,32,256]{4,1,3,2,0:T(8,128)} %get-tuple-element.345, f32[3,8,16,16]{3,2,0,1:T(8,128)S(1)} %get-tuple-element.344, s32[]{:T(128)} %get-tuple-element.335), kind=kOutput, calls=%fused_computation.5.clone.1 | convolution fusion | flops 610271232 | bytes 38035460 | tf_op jit(solution)/shard_map/while/body/eval_jaxpr/mij,mjxyz->mixyz/dot_general | solution.py:81
  756.4 19.1 %multiply_add_fusion.5 = f32[3,16,8,32,256]{4,1,3,2,0:T(8,128)} fusion(f32[3,16,8,32,256]{4,1,3,2,0:T(8,128)} %get-tuple-element.336, f32[8,32,256]{2,1,0:T(8,128)S(1)} %dynamic-slice_bitcast_fusion.5, f32[3,16,8,32,256]{4,1,3,2,0:T(8,128)} %get-tuple-element.345, f32[3,8,16,16]{3,2,0,1:T(8,128)S(1)} %get-tuple-element.344, s32[]{:T(128)} %get-tuple-element.335), kind=kOutput, calls=%fused_computation.5.clone.1 | convolution fusion | flops 610271232 | bytes 38035460 | tf_op jit(solution)/shard_map/while/body/eval_jaxpr/mij,mjxyz->mixyz/dot_general | solution.py:81
  775.5 19.1 %multiply_add_fusion.5 = f32[3,16,8,32,256]{4,1,3,2,0:T(8,128)} fusion(f32[3,16,8,32,256]{4,1,3,2,0:T(8,128)} %get-tuple-element.336, f32[8,32,256]{2,1,0:T(8,128)S(1)} %dynamic-slice_bitcast_fusion.5, f32[3,16,8,32,256]{4,1,3,2,0:T(8,128)} %get-tuple-element.345, f32[3,8,16,16]{3,2,0,1:T(8,128)S(1)} %get-tuple-element.344, s32[]{:T(128)} %get-tuple-element.335), kind=kOutput, calls=%fused_computation.5.clone.1 | convolution fusion | flops 610271232 | bytes 38035460 | tf_op jit(solution)/shard_map/while/body/eval_jaxpr/mij,mjxyz->mixyz/dot_general | solution.py:81
  794.6 19.1 %multiply_add_fusion.5 = f32[3,16,8,32,256]{4,1,3,2,0:T(8,128)} fusion(f32[3,16,8,32,256]{4,1,3,2,0:T(8,128)} %get-tuple-element.336, f32[8,32,256]{2,1,0:T(8,128)S(1)} %dynamic-slice_bitcast_fusion.5, f32[3,16,8,32,256]{4,1,3,2,0:T(8,128)} %get-tuple-element.345, f32[3,8,16,16]{3,2,0,1:T(8,128)S(1)} %get-tuple-element.344, s32[]{:T(128)} %get-tuple-element.335), kind=kOutput, calls=%fused_computation.5.clone.1 | convolution fusion | flops 610271232 | bytes 38035460 | tf_op jit(solution)/shard_map/while/body/eval_jaxpr/mij,mjxyz->mixyz/dot_general | solution.py:81
  813.7 19.1 %multiply_add_fusion.5 = f32[3,16,8,32,256]{4,1,3,2,0:T(8,128)} fusion(f32[3,16,8,32,256]{4,1,3,2,0:T(8,128)} %get-tuple-element.336, f32[8,32,256]{2,1,0:T(8,128)S(1)} %dynamic-slice_bitcast_fusion.5, f32[3,16,8,32,256]{4,1,3,2,0:T(8,128)} %get-tuple-element.345, f32[3,8,16,16]{3,2,0,1:T(8,128)S(1)} %get-tuple-element.344, s32[]{:T(128)} %get-tuple-element.335), kind=kOutput, calls=%fused_computation.5.clone.1 | convolution fusion | flops 610271232 | bytes 38035460 | tf_op jit(solution)/shard_map/while/body/eval_jaxpr/mij,mjxyz->mixyz/dot_general | solution.py:81
  832.8 13.4 %fusion.36 = f32[3,16,8,32,256]{4,3,2,0,1:T(8,128)S(1)} fusion(f32[3,16,8,32,256]{4,3,2,0,1:T(8,128)} %copy-done.2, f32[3,16,8,32,256]{4,1,3,2,0:T(8,128)} %get-tuple-element.194, f32[8,32,256]{2,1,0:T(8,128)S(1)} %fusion.40), kind=kLoop, calls=%fused_computation.61 | loop fusion | flops 6291456 | bytes 38010880 | tf_op jit(solution)/shard_map/add | solution.py:114
  846.2 110.0 %all_to_all.37 = f32[3,16,8,32,256]{4,3,2,0,1:T(8,128)} all-to-all(f32[3,16,8,32,256]{4,3,2,0,1:T(8,128)S(1)} %fusion.36), channel_id=1, replica_groups=mesh['space'=16,'mode'=2] {'mode'}, dimensions={1} | all-to-all | bytes 25165824 | tf_op jit(solution)/shard_map/all_to_all | solution.py:115
  956.3 12.2 %copy.22 = f32[3,8,8,2,32,256]{5,4,3,2,1,0:T(8,128)} copy(f32[3,8,8,2,32,256]{5,4,2,0,1,3:T(8,128)} %bitcast.54) | data formatting | bytes 25165824 | tf_op jit(solution)/shard_map/all_to_all | solution.py:115
  968.4 0.0 copy-done.1
  (31 shorter events, 0.4 us)
Async XLA Ops:
  0.0 199.1 %copy-start = (s32[8,64,256]{2,1,0:T(8,128)S(1)}, s32[8,64,256]{2,1,0:T(8,128)}, u32[]{:S(2)}) copy-start(s32[8,64,256]{2,1,0:T(8,128)} %param.15) | copy-start | bytes 1572868
  185.6 12.3 %copy-start.9 = (f32[16,16,16,1]{2,1,3,0:T(8,128)S(1)}, f32[16,16,16,1]{2,1,3,0:T(8,128)}, u32[]{:S(2)}) copy-start(f32[16,16,16,1]{2,1,3,0:T(8,128)} %constant.101) | copy-start | bytes 49156
  185.6 12.4 %copy-start.10 = (f32[3,8,16]{2,1,0:T(8,128)S(1)}, f32[3,8,16]{2,1,0:T(8,128)}, u32[]{:S(2)}) copy-start(f32[3,8,16]{2,1,0:T(8,128)} %param.14) | copy-start | bytes 4612
  185.6 13.5 %copy-start.7 = (f32[8,64,256]{2,1,0:T(8,128)S(1)}, f32[8,64,256]{2,1,0:T(8,128)}, u32[]{:S(2)}) copy-start(f32[8,64,256]{2,1,0:T(8,128)} %param.12) | copy-start | bytes 1572868
  185.6 13.5 %copy-start.8 = (f32[8,64,256]{2,1,0:T(8,128)S(1)}, f32[8,64,256]{2,1,0:T(8,128)}, u32[]{:S(2)}) copy-start(f32[8,64,256]{2,1,0:T(8,128)} %param.13) | copy-start | bytes 1572868
  185.6 21.5 %copy-start.6 = (s32[8,64,256]{2,1,0:T(8,128)S(1)}, s32[8,64,256]{2,1,0:T(8,128)}, u32[]{:S(2)}) copy-start(s32[8,64,256]{2,1,0:T(8,128)} %param.16) | copy-start | bytes 1572868
  192.4 72.6 %collective-permute-start = (f32[3,16,2,32,256]{4,3,2,0,1:T(8,128)}, f32[3,16,2,32,256]{4,3,2,0,1:T(8,128)}, u32[]{:S(2)}, u32[]{:S(2)}) collective-permute-start(f32[3,16,2,32,256]{4,3,2,0,1:T(8,128)} %get-tuple-element.243), channel_id=1, source_target_pairs={{0,2},{2,4},{4,6},{6,8},{8,10},{10,12},{12,14},{14,16},{16,18},{18... | collective-permute-start | bytes 9437192 | tf_op jit(solution)/shard_map/ppermute | solution.py:19
  194.3 70.7 %collective-permute-start.1 = (f32[3,16,2,32,256]{4,3,2,0,1:T(8,128)}, f32[3,16,2,32,256]{4,3,2,0,1:T(8,128)}, u32[]{:S(2)}, u32[]{:S(2)}) collective-permute-start(f32[3,16,2,32,256]{4,3,2,0,1:T(8,128)} %get-tuple-element.244), channel_id=1, source_target_pairs={{2,0},{4,2},{6,4},{8,6},{10,8},{12,10},{14,12},{16,14},{18,16},{20... | collective-permute-start | bytes 9437192 | tf_op jit(solution)/shard_map/ppermute | solution.py:20
  202.8 10.7 %collective-permute-start.2 = (f32[3,16,8,1,256]{4,3,2,0,1:T(1,128)S(1)}, f32[3,16,8,1,256]{4,3,2,0,1:T(1,128)}, u32[]{:S(2)}, u32[]{:S(2)}) collective-permute-start(f32[3,16,8,1,256]{4,3,2,0,1:T(1,128)S(1)} %get-tuple-element.245), channel_id=1, source_target_pairs={{0,1},{2,3},{4,5},{6,7},{8,9},{10,11},{12,13},{14,15},{16,17},{18,... | collective-permute-start | bytes 1179656 | tf_op jit(solution)/shard_map/ppermute | solution.py:19
  205.8 12.7 %collective-permute-start.3 = (f32[3,16,8,1,256]{4,3,2,0,1:T(1,128)S(1)}, f32[3,16,8,1,256]{4,3,2,0,1:T(1,128)}, u32[]{:S(2)}, u32[]{:S(2)}) collective-permute-start(f32[3,16,8,1,256]{4,3,2,0,1:T(1,128)S(1)} %get-tuple-element.246), channel_id=1, source_target_pairs={{1,0},{3,2},{5,4},{7,6},{9,8},{11,10},{13,12},{15,14},{17,16},{19,... | collective-permute-start | bytes 1179656 | tf_op jit(solution)/shard_map/ppermute | solution.py:20
  518.2 6.7 copy-start.2
  519.3 72.3 %collective-permute-start.4 = (f32[3,16,2,32,256]{4,3,2,0,1:T(8,128)S(1)}, f32[3,16,2,32,256]{4,3,2,0,1:T(8,128)S(1)}, u32[]{:S(2)}, u32[]{:S(2)}) collective-permute-start(f32[3,16,2,32,256]{4,3,2,0,1:T(8,128)S(1)} %get-tuple-element.239), channel_id=1, source_target_pairs={{0,2},{2,4},{4,6},{6,8},{8,10},{10,12},{12,14},{14,16},{16,18},{18... | collective-permute-start | bytes 9437192 | tf_op jit(solution)/shard_map/ppermute | solution.py:19
  521.3 72.1 %collective-permute-start.5 = (f32[3,16,2,32,256]{4,3,2,0,1:T(8,128)S(1)}, f32[3,16,2,32,256]{4,3,2,0,1:T(8,128)}, u32[]{:S(2)}, u32[]{:S(2)}) collective-permute-start(f32[3,16,2,32,256]{4,3,2,0,1:T(8,128)S(1)} %get-tuple-element.240), channel_id=1, source_target_pairs={{2,0},{4,2},{6,4},{8,6},{10,8},{12,10},{14,12},{16,14},{18,16},{20... | collective-permute-start | bytes 9437192 | tf_op jit(solution)/shard_map/ppermute | solution.py:20
  525.5 9.5 collective-permute-start.6
  527.8 11.4 %collective-permute-start.7 = (f32[3,16,8,1,256]{4,3,2,0,1:T(1,128)S(1)}, f32[3,16,8,1,256]{4,3,2,0,1:T(1,128)S(1)}, u32[]{:S(2)}, u32[]{:S(2)}) collective-permute-start(f32[3,16,8,1,256]{4,3,2,0,1:T(1,128)S(1)} %get-tuple-element.242), channel_id=1, source_target_pairs={{1,0},{3,2},{5,4},{7,6},{9,8},{11,10},{13,12},{15,14},{17,16},{19,... | collective-permute-start | bytes 1179656 | tf_op jit(solution)/shard_map/ppermute | solution.py:20
  535.0 56.6 %copy-start.4 = (f32[3,16,8,1,256]{4,3,2,0,1:T(1,128)}, f32[3,16,8,1,256]{4,3,2,0,1:T(1,128)S(1)}, u32[]{:S(2)}) copy-start(f32[3,16,8,1,256]{4,3,2,0,1:T(1,128)S(1)} %collective-permute-done.6) | copy-start | bytes 1179652
  539.2 52.5 %copy-start.5 = (f32[3,16,8,1,256]{4,3,2,0,1:T(1,128)}, f32[3,16,8,1,256]{4,3,2,0,1:T(1,128)S(1)}, u32[]{:S(2)}) copy-start(f32[3,16,8,1,256]{4,3,2,0,1:T(1,128)S(1)} %collective-permute-done.7) | copy-start | bytes 1179652
  591.6 1.7 copy-start.3
  956.3 12.2 %copy-start.1 = (s32[8,64,256]{2,1,0:T(8,128)S(1)}, s32[8,64,256]{2,1,0:T(8,128)}, u32[]{:S(2)}) copy-start(s32[8,64,256]{2,1,0:T(8,128)} %param.15) | copy-start | bytes 1572868
where the time goes:
time: 975 us; the launch traced here: 969 us
  matrix products  306 us (31%)
  blocking collectives  262 us (27%)
  local copies, waits for them, and re-layouts  141 us (14%)
  waiting for transfers between devices  120 us (12%)
  other arithmetic  119 us (12%)
  starting transfers between devices  18.9 us (2%)
    dot_general x16, matrix products, add_class(): jnp.einsum('mij,mjxyz->mixyz', matrix, piece, precision=lax.Precision.HIG...  305 us
    all_to_all x1, blocking collectives, on_device(): lax.all_to_all(field, 'mode', split_axis=3, concat_axis=1, tiled=True)  152 us
    ppermute x4, waiting for transfers between devices, padded(): before = lax.ppermute(last, axis, up)  111 us
    all_to_all x1, blocking collectives, on_device(): lax.all_to_all(state, 'mode', split_axis=1, concat_axis=3, tiled=True)  110 us
    mul x2, other arithmetic, on_device(): MOBILE_BASE * operated  91.7 us
    while x5, local copies, waits for them, and re-layouts, class_terms(): return lax.fori_loop(0, class_mats.shape[1], add_class, total)  81.4 us
    add x2, other arithmetic, on_device(): state = state + TIME_STEP * movable_here[None, None] * coupled  26.9 us
  transfers between devices with their start and end apart: 8, of which 6 were waited for; matrix products, arithmetic and copies ran while one was open for 1% of the time, Pallas kernels for 0%

commit v1 on v0

--- a/solution.py
+++ b/solution.py
@@ -112,7 +112,10 @@
         operated = stencil(x_padded, y_padded, speed_here, spread_here)
         coupled = class_terms(MOBILE_BASE * operated, class_mats, operated, picks_here)
         state = state + TIME_STEP * movable_here[None, None] * coupled
-    state = lax.all_to_all(state, "mode", split_axis=1, concat_axis=3, tiled=True)
+    state = jnp.concatenate(
+        lax.all_to_all(jnp.stack(jnp.split(state, lax.axis_size("mode"), axis=1)), "mode", 0, 0),
+        axis=3,
+    )
     return state
 
 

time: 975 us -> 932 us (0.956)
  local copies, waits for them, and re-layouts: 141 us -> 63.9 us
  other arithmetic: 119 us -> 139 us
  blocking collectives: 262 us -> 273 us
    while x5 -> x1, local copies, waits for them, and re-layouts: 81.4 us -> 0.05 us  [class_terms(): return lax.fori_loop(0, class_mats.shape[1], add_class, total)]
    reshape x0 -> x1, local copies, waits for them, and re-layouts: none -> 13.2 us  [on_device(): jnp.concatenate(lax.all_to_all(jnp.stack(jnp.split(state, lax.axis_size('...]
    all_to_all x1 -> x0, local copies, waits for them, and re-layouts: 12.2 us -> none  [on_device(): lax.all_to_all(state, 'mode', split_axis=1, concat_axis=3, tiled=True)]
    another operation x0 -> x1, other arithmetic: none -> 10.8 us  [on_device(): jnp.stack(jnp.split(state, lax.axis_size('mode'), axis=1))]
    another operation x0 -> x1, local copies, waits for them, and re-layouts: none -> 10.5 us  [on_device(): jnp.stack(jnp.split(state, lax.axis_size('mode'), axis=1))]
    mul x2, other arithmetic: 91.7 us -> 102 us  [on_device(): MOBILE_BASE * operated]
    all_to_all x1, blocking collectives: 110 us -> 120 us  [on_device(): lax.all_to_all(jnp.stack(jnp.split(state, lax.axis_size('mode'), axis=1))...]
  transfers between devices with their start and end apart: 8 -> 8, of which waited for: 6 -> 6; matrix products, arithmetic and copies ran while one was open for 1% -> 0% of each run, Pallas kernels for 0% -> 0%
where the time goes in v1:
time: 932 us; the launch traced here: 925 us
  matrix products  306 us (33%)
  blocking collectives  273 us (29%)
  other arithmetic  139 us (15%)
  waiting for transfers between devices  123 us (13%)
  local copies, waits for them, and re-layouts  63.9 us (7%)
  starting transfers between devices  19.1 us (2%)
    dot_general x16, matrix products, add_class(): jnp.einsum('mij,mjxyz->mixyz', matrix, piece, precision=lax.Precision.HIG...  305 us
    all_to_all x1, blocking collectives, on_device(): lax.all_to_all(field, 'mode', split_axis=3, concat_axis=1, tiled=True)  153 us
    all_to_all x1, blocking collectives, on_device(): lax.all_to_all(jnp.stack(jnp.split(state, lax.axis_size('mode'), axis=1))...  120 us
    ppermute x4, waiting for transfers between devices, padded(): before = lax.ppermute(last, axis, up)  114 us
    mul x2, other arithmetic, on_device(): MOBILE_BASE * operated  102 us
    add x2, other arithmetic, on_device(): state = state + TIME_STEP * movable_here[None, None] * coupled  25.9 us
  transfers between devices with their start and end apart: 8, of which 6 were waited for; matrix products, arithmetic and copies ran while one was open for 0% of the time, Pallas kernels for 0%

profile of v1, /device:TPU:10, one launch (start us, length us, event | category | flops | bytes accessed | tf_op | source)
XLA Modules:
  0.0 924.9 jit_solution(2315235995513681073)
XLA Ops:
  0.0 0.0 copy-start
  0.0 16.7 %copy.12 = f32[3,8,8,64,256]{4,2,1,0,3:T(8,128)} copy(f32[3,8,8,64,256]{4,3,2,1,0:T(8,128)} %param.11) | data formatting | bytes 25165824 | tf_op args[0]
  16.7 152.6 %all_to_all.23 = f32[3,8,8,64,256]{4,2,1,0,3:T(8,128)} all-to-all(f32[3,8,8,64,256]{4,2,1,0,3:T(8,128)} %copy.12), channel_id=1, replica_groups=mesh['space'=16,'mode'=2] {'mode'}, dimensions={3} | all-to-all | bytes 25165824 | tf_op jit(solution)/shard_map/all_to_all | solution.py:104
  169.3 13.1 %copy.23 = f32[3,2,8,8,32,256]{5,2,1,4,3,0:T(8,128)} copy(f32[3,2,8,8,32,256]{5,3,2,0,4,1:T(8,128)} %bitcast.55) | data formatting | bytes 25165824 | tf_op jit(solution)/shard_map/all_to_all | solution.py:104
  182.4 0.0 copy-start.6
  182.5 6.3 fusion.44
  188.7 1.9 collective-permute-start
  190.6 3.6 collective-permute-start.1
  194.3 0.0 copy-done.9
  194.3 0.0 copy-done.10
  194.3 1.0 convolution_bitcast_fusion
  195.4 0.0 copy-done
  195.4 0.0 copy-done.7
  195.5 0.0 copy-done.8
  195.5 0.1 dynamic-slice_multiply_fusion
  195.5 1.2 fusion.45
  196.7 3.0 collective-permute-start.2
  199.7 1.3 collective-permute-start.3
  201.0 0.0 copy-done.6
  201.0 0.3 fusion.36
  201.3 6.1 collective-permute-done.2
  207.4 5.0 collective-permute-done.3
  212.3 49.0 %collective-permute-done = f32[3,16,2,32,256]{4,1,3,2,0:T(8,128)} collective-permute-done((f32[3,16,2,32,256]{4,1,3,2,0:T(8,128)}, f32[3,16,2,32,256]{4,1,3,2,0:T(8,128)}, u32[]{:S(2)}, u32[]{:S(2)}) %collective-permute-start) | collective-permute-done | bytes 3145760 | tf_op jit(solution)/shard_map/ppermute | solution.py:19
  261.3 0.0 collective-permute-done.1
  261.3 51.2 %broadcast_multiply_fusion.1 = (f32[3,16,8,32,256]{4,1,3,2,0:T(8,128)}, f32[3,16,8,32,256]{4,1,3,2,0:T(8,128)}) fusion(f32[8,32,256]{2,1,0:T(8,128)S(1)} %get-tuple-element.249, f32[3,16,8,32,256]{4,1,3,2,0:T(8,128)} %bitcast.59, f32[3,16,8,1,256]{4,1,3,2,0:T(8,128)} %collective-permute-done.3, f32[3,16,8,1,256]{4,1,3,2,0:T(8,128)} %collective-permute-done.2, ...), kind=kLoop, calls=%fused_computation.67 | loop fusion | flops 91226112 | bytes 45350912 | tf_op jit(solution)/shard_map/mul | solution.py:113
  312.5 152.7 %while.26 = (s32[]{:T(128)}, f32[3,16,8,32,256]{4,1,3,2,0:T(8,128)}, f32[8,8,32,256]{3,2,1,0:T(8,128)S(1)}, f32[3,8,16,16]{3,2,0,1:T(8,128)S(1)}, f32[3,16,8,32,256]{4,1,3,2,0:T(8,128)}, /*index=5*/s32[]{:T(128)}) while((s32[]{:T(128)}, f32[3,16,8,32,256]{4,1,3,2,0:T(8,128)}, f32[8,8,32,256]{3,2,1,0:T(8,128)S(1)}, ...), condition=%wide.region_1.2_spmd, body=%wide.region_0.1_spmd.sunk | while | flops 610271232 | bytes 38559820 | solution.py:85
  312.5 19.1 %multiply_add_fusion.6 = f32[3,16,8,32,256]{4,1,3,2,0:T(8,128)} fusion(f32[3,16,8,32,256]{4,1,3,2,0:T(8,128)} %get-tuple-element.320, f32[8,32,256]{2,1,0:T(8,128)S(1)} %dynamic-slice_bitcast_fusion.4, f32[3,16,8,32,256]{4,1,3,2,0:T(8,128)} %get-tuple-element.329, f32[3,8,16,16]{3,2,0,1:T(8,128)S(1)} %get-tuple-element.328, s32[]{:T(128)} %get-tuple-element.319), kind=kOutput, calls=%fused_computation.clone.1 | convolution fusion | flops 610271232 | bytes 38035460 | tf_op jit(solution)/shard_map/while/body/eval_jaxpr/mij,mjxyz->mixyz/dot_general | solution.py:81
  331.6 19.1 %multiply_add_fusion.6 = f32[3,16,8,32,256]{4,1,3,2,0:T(8,128)} fusion(f32[3,16,8,32,256]{4,1,3,2,0:T(8,128)} %get-tuple-element.320, f32[8,32,256]{2,1,0:T(8,128)S(1)} %dynamic-slice_bitcast_fusion.4, f32[3,16,8,32,256]{4,1,3,2,0:T(8,128)} %get-tuple-element.329, f32[3,8,16,16]{3,2,0,1:T(8,128)S(1)} %get-tuple-element.328, s32[]{:T(128)} %get-tuple-element.319), kind=kOutput, calls=%fused_computation.clone.1 | convolution fusion | flops 610271232 | bytes 38035460 | tf_op jit(solution)/shard_map/while/body/eval_jaxpr/mij,mjxyz->mixyz/dot_general | solution.py:81
  350.7 19.1 %multiply_add_fusion.6 = f32[3,16,8,32,256]{4,1,3,2,0:T(8,128)} fusion(f32[3,16,8,32,256]{4,1,3,2,0:T(8,128)} %get-tuple-element.320, f32[8,32,256]{2,1,0:T(8,128)S(1)} %dynamic-slice_bitcast_fusion.4, f32[3,16,8,32,256]{4,1,3,2,0:T(8,128)} %get-tuple-element.329, f32[3,8,16,16]{3,2,0,1:T(8,128)S(1)} %get-tuple-element.328, s32[]{:T(128)} %get-tuple-element.319), kind=kOutput, calls=%fused_computation.clone.1 | convolution fusion | flops 610271232 | bytes 38035460 | tf_op jit(solution)/shard_map/while/body/eval_jaxpr/mij,mjxyz->mixyz/dot_general | solution.py:81
  369.8 19.1 %multiply_add_fusion.6 = f32[3,16,8,32,256]{4,1,3,2,0:T(8,128)} fusion(f32[3,16,8,32,256]{4,1,3,2,0:T(8,128)} %get-tuple-element.320, f32[8,32,256]{2,1,0:T(8,128)S(1)} %dynamic-slice_bitcast_fusion.4, f32[3,16,8,32,256]{4,1,3,2,0:T(8,128)} %get-tuple-element.329, f32[3,8,16,16]{3,2,0,1:T(8,128)S(1)} %get-tuple-element.328, s32[]{:T(128)} %get-tuple-element.319), kind=kOutput, calls=%fused_computation.clone.1 | convolution fusion | flops 610271232 | bytes 38035460 | tf_op jit(solution)/shard_map/while/body/eval_jaxpr/mij,mjxyz->mixyz/dot_general | solution.py:81
  388.9 19.1 %multiply_add_fusion.6 = f32[3,16,8,32,256]{4,1,3,2,0:T(8,128)} fusion(f32[3,16,8,32,256]{4,1,3,2,0:T(8,128)} %get-tuple-element.320, f32[8,32,256]{2,1,0:T(8,128)S(1)} %dynamic-slice_bitcast_fusion.4, f32[3,16,8,32,256]{4,1,3,2,0:T(8,128)} %get-tuple-element.329, f32[3,8,16,16]{3,2,0,1:T(8,128)S(1)} %get-tuple-element.328, s32[]{:T(128)} %get-tuple-element.319), kind=kOutput, calls=%fused_computation.clone.1 | convolution fusion | flops 610271232 | bytes 38035460 | tf_op jit(solution)/shard_map/while/body/eval_jaxpr/mij,mjxyz->mixyz/dot_general | solution.py:81
  408.0 19.1 %multiply_add_fusion.6 = f32[3,16,8,32,256]{4,1,3,2,0:T(8,128)} fusion(f32[3,16,8,32,256]{4,1,3,2,0:T(8,128)} %get-tuple-element.320, f32[8,32,256]{2,1,0:T(8,128)S(1)} %dynamic-slice_bitcast_fusion.4, f32[3,16,8,32,256]{4,1,3,2,0:T(8,128)} %get-tuple-element.329, f32[3,8,16,16]{3,2,0,1:T(8,128)S(1)} %get-tuple-element.328, s32[]{:T(128)} %get-tuple-element.319), kind=kOutput, calls=%fused_computation.clone.1 | convolution fusion | flops 610271232 | bytes 38035460 | tf_op jit(solution)/shard_map/while/body/eval_jaxpr/mij,mjxyz->mixyz/dot_general | solution.py:81
  427.1 19.1 %multiply_add_fusion.6 = f32[3,16,8,32,256]{4,1,3,2,0:T(8,128)} fusion(f32[3,16,8,32,256]{4,1,3,2,0:T(8,128)} %get-tuple-element.320, f32[8,32,256]{2,1,0:T(8,128)S(1)} %dynamic-slice_bitcast_fusion.4, f32[3,16,8,32,256]{4,1,3,2,0:T(8,128)} %get-tuple-element.329, f32[3,8,16,16]{3,2,0,1:T(8,128)S(1)} %get-tuple-element.328, s32[]{:T(128)} %get-tuple-element.319), kind=kOutput, calls=%fused_computation.clone.1 | convolution fusion | flops 610271232 | bytes 38035460 | tf_op jit(solution)/shard_map/while/body/eval_jaxpr/mij,mjxyz->mixyz/dot_general | solution.py:81
  446.2 19.1 %multiply_add_fusion.6 = f32[3,16,8,32,256]{4,1,3,2,0:T(8,128)} fusion(f32[3,16,8,32,256]{4,1,3,2,0:T(8,128)} %get-tuple-element.320, f32[8,32,256]{2,1,0:T(8,128)S(1)} %dynamic-slice_bitcast_fusion.4, f32[3,16,8,32,256]{4,1,3,2,0:T(8,128)} %get-tuple-element.329, f32[3,8,16,16]{3,2,0,1:T(8,128)S(1)} %get-tuple-element.328, s32[]{:T(128)} %get-tuple-element.319), kind=kOutput, calls=%fused_computation.clone.1 | convolution fusion | flops 610271232 | bytes 38035460 | tf_op jit(solution)/shard_map/while/body/eval_jaxpr/mij,mjxyz->mixyz/dot_general | solution.py:81
  465.2 11.3 %multiply_add_fusion.3 = f32[3,16,8,32,256]{4,1,3,2,0:T(8,128)S(1)} fusion(f32[3,16,8,32,256]{4,1,3,2,0:T(8,128)} %get-tuple-element.193, f32[8,32,256]{2,1,0:T(8,128)S(1)} %fusion.38, f32[3,2,8,8,32,256]{5,3,2,0,4,1:T(8,128)} %bitcast.56), kind=kLoop, calls=%fused_computation.63 | loop fusion | flops 6291456 | bytes 38010880 | tf_op jit(solution)/shard_map/add | solution.py:114
  476.5 0.0 copy-start.2
  476.5 0.8 fusion.42
  477.3 2.1 collective-permute-start.4
  479.4 3.6 collective-permute-start.5
  483.1 0.0 copy-done.2
  483.1 0.1 fusion.43
  483.1 2.2 collective-permute-start.6
  485.4 1.3 collective-permute-start.7
  486.7 6.0 collective-permute-done.6
  492.7 4.1 collective-permute-done.7
  496.8 52.8 %collective-permute-done.4 = f32[3,16,2,32,256]{4,1,3,2,0:T(8,128)S(1)} collective-permute-done((f32[3,16,2,32,256]{4,1,3,2,0:T(8,128)S(1)}, f32[3,16,2,32,256]{4,1,3,2,0:T(8,128)S(1)}, u32[]{:S(2)}, u32[]{:S(2)}) %collective-permute-start.4) | collective-permute-done | bytes 3145760 | tf_op jit(solution)/shard_map/ppermute | solution.py:19
  549.6 0.0 copy-done.5
  549.6 1.7 copy-done.3
  551.3 0.0 collective-permute-done.5
  551.3 51.0 %broadcast_multiply_fusion = (f32[3,16,8,32,256]{4,1,3,2,0:T(8,128)}, f32[3,16,8,32,256]{4,1,3,2,0:T(8,128)}) fusion(f32[8,32,256]{2,1,0:T(8,128)S(1)} %get-tuple-element.249, f32[3,16,8,32,256]{4,1,3,2,0:T(8,128)} %copy-done.2, f32[3,16,8,1,256]{4,1,3,2,0:T(8,128)} %copy-done.5, f32[3,16,8,1,256]{4,1,3,2,0:T(8,128)} %copy-done.4, ...), kind=kLoop, calls=%fused_computation.66 | loop fusion | flops 91226112 | bytes 45350912 | tf_op jit(solution)/shard_map/mul | solution.py:113
  602.3 152.9 %while.27 = (s32[]{:T(128)}, f32[3,16,8,32,256]{4,1,3,2,0:T(8,128)}, f32[8,8,32,256]{3,2,1,0:T(8,128)S(1)}, f32[3,8,16,16]{3,2,0,1:T(8,128)S(1)}, f32[3,16,8,32,256]{4,1,3,2,0:T(8,128)}, /*index=5*/s32[]{:T(128)}) while((s32[]{:T(128)}, f32[3,16,8,32,256]{4,1,3,2,0:T(8,128)}, f32[8,8,32,256]{3,2,1,0:T(8,128)S(1)}, ...), condition=%wide.region_3.4_spmd, body=%wide.region_2.3_spmd.sunk | while | flops 610271232 | bytes 38559820 | solution.py:85
  602.3 19.1 %multiply_add_fusion.7 = f32[3,16,8,32,256]{4,1,3,2,0:T(8,128)} fusion(f32[3,16,8,32,256]{4,1,3,2,0:T(8,128)} %get-tuple-element.338, f32[8,32,256]{2,1,0:T(8,128)S(1)} %dynamic-slice_bitcast_fusion.5, f32[3,16,8,32,256]{4,1,3,2,0:T(8,128)} %get-tuple-element.347, f32[3,8,16,16]{3,2,0,1:T(8,128)S(1)} %get-tuple-element.346, s32[]{:T(128)} %get-tuple-element.337), kind=kOutput, calls=%fused_computation.5.clone.1 | convolution fusion | flops 610271232 | bytes 38035460 | tf_op jit(solution)/shard_map/while/body/eval_jaxpr/mij,mjxyz->mixyz/dot_general | solution.py:81
  621.4 19.1 %multiply_add_fusion.7 = f32[3,16,8,32,256]{4,1,3,2,0:T(8,128)} fusion(f32[3,16,8,32,256]{4,1,3,2,0:T(8,128)} %get-tuple-element.338, f32[8,32,256]{2,1,0:T(8,128)S(1)} %dynamic-slice_bitcast_fusion.5, f32[3,16,8,32,256]{4,1,3,2,0:T(8,128)} %get-tuple-element.347, f32[3,8,16,16]{3,2,0,1:T(8,128)S(1)} %get-tuple-element.346, s32[]{:T(128)} %get-tuple-element.337), kind=kOutput, calls=%fused_computation.5.clone.1 | convolution fusion | flops 610271232 | bytes 38035460 | tf_op jit(solution)/shard_map/while/body/eval_jaxpr/mij,mjxyz->mixyz/dot_general | solution.py:81
  640.5 19.1 %multiply_add_fusion.7 = f32[3,16,8,32,256]{4,1,3,2,0:T(8,128)} fusion(f32[3,16,8,32,256]{4,1,3,2,0:T(8,128)} %get-tuple-element.338, f32[8,32,256]{2,1,0:T(8,128)S(1)} %dynamic-slice_bitcast_fusion.5, f32[3,16,8,32,256]{4,1,3,2,0:T(8,128)} %get-tuple-element.347, f32[3,8,16,16]{3,2,0,1:T(8,128)S(1)} %get-tuple-element.346, s32[]{:T(128)} %get-tuple-element.337), kind=kOutput, calls=%fused_computation.5.clone.1 | convolution fusion | flops 610271232 | bytes 38035460 | tf_op jit(solution)/shard_map/while/body/eval_jaxpr/mij,mjxyz->mixyz/dot_general | solution.py:81
  659.7 19.1 %multiply_add_fusion.7 = f32[3,16,8,32,256]{4,1,3,2,0:T(8,128)} fusion(f32[3,16,8,32,256]{4,1,3,2,0:T(8,128)} %get-tuple-element.338, f32[8,32,256]{2,1,0:T(8,128)S(1)} %dynamic-slice_bitcast_fusion.5, f32[3,16,8,32,256]{4,1,3,2,0:T(8,128)} %get-tuple-element.347, f32[3,8,16,16]{3,2,0,1:T(8,128)S(1)} %get-tuple-element.346, s32[]{:T(128)} %get-tuple-element.337), kind=kOutput, calls=%fused_computation.5.clone.1 | convolution fusion | flops 610271232 | bytes 38035460 | tf_op jit(solution)/shard_map/while/body/eval_jaxpr/mij,mjxyz->mixyz/dot_general | solution.py:81
  678.8 19.1 %multiply_add_fusion.7 = f32[3,16,8,32,256]{4,1,3,2,0:T(8,128)} fusion(f32[3,16,8,32,256]{4,1,3,2,0:T(8,128)} %get-tuple-element.338, f32[8,32,256]{2,1,0:T(8,128)S(1)} %dynamic-slice_bitcast_fusion.5, f32[3,16,8,32,256]{4,1,3,2,0:T(8,128)} %get-tuple-element.347, f32[3,8,16,16]{3,2,0,1:T(8,128)S(1)} %get-tuple-element.346, s32[]{:T(128)} %get-tuple-element.337), kind=kOutput, calls=%fused_computation.5.clone.1 | convolution fusion | flops 610271232 | bytes 38035460 | tf_op jit(solution)/shard_map/while/body/eval_jaxpr/mij,mjxyz->mixyz/dot_general | solution.py:81
  697.9 19.1 %multiply_add_fusion.7 = f32[3,16,8,32,256]{4,1,3,2,0:T(8,128)} fusion(f32[3,16,8,32,256]{4,1,3,2,0:T(8,128)} %get-tuple-element.338, f32[8,32,256]{2,1,0:T(8,128)S(1)} %dynamic-slice_bitcast_fusion.5, f32[3,16,8,32,256]{4,1,3,2,0:T(8,128)} %get-tuple-element.347, f32[3,8,16,16]{3,2,0,1:T(8,128)S(1)} %get-tuple-element.346, s32[]{:T(128)} %get-tuple-element.337), kind=kOutput, calls=%fused_computation.5.clone.1 | convolution fusion | flops 610271232 | bytes 38035460 | tf_op jit(solution)/shard_map/while/body/eval_jaxpr/mij,mjxyz->mixyz/dot_general | solution.py:81
  717.0 19.1 %multiply_add_fusion.7 = f32[3,16,8,32,256]{4,1,3,2,0:T(8,128)} fusion(f32[3,16,8,32,256]{4,1,3,2,0:T(8,128)} %get-tuple-element.338, f32[8,32,256]{2,1,0:T(8,128)S(1)} %dynamic-slice_bitcast_fusion.5, f32[3,16,8,32,256]{4,1,3,2,0:T(8,128)} %get-tuple-element.347, f32[3,8,16,16]{3,2,0,1:T(8,128)S(1)} %get-tuple-element.346, s32[]{:T(128)} %get-tuple-element.337), kind=kOutput, calls=%fused_computation.5.clone.1 | convolution fusion | flops 610271232 | bytes 38035460 | tf_op jit(solution)/shard_map/while/body/eval_jaxpr/mij,mjxyz->mixyz/dot_general | solution.py:81
  736.1 19.1 %multiply_add_fusion.7 = f32[3,16,8,32,256]{4,1,3,2,0:T(8,128)} fusion(f32[3,16,8,32,256]{4,1,3,2,0:T(8,128)} %get-tuple-element.338, f32[8,32,256]{2,1,0:T(8,128)S(1)} %dynamic-slice_bitcast_fusion.5, f32[3,16,8,32,256]{4,1,3,2,0:T(8,128)} %get-tuple-element.347, f32[3,8,16,16]{3,2,0,1:T(8,128)S(1)} %get-tuple-element.346, s32[]{:T(128)} %get-tuple-element.337), kind=kOutput, calls=%fused_computation.5.clone.1 | convolution fusion | flops 610271232 | bytes 38035460 | tf_op jit(solution)/shard_map/while/body/eval_jaxpr/mij,mjxyz->mixyz/dot_general | solution.py:81
  755.2 14.6 %multiply_add_fusion.2 = f32[3,16,8,32,256]{4,1,3,2,0:T(8,128)} fusion(f32[3,16,8,32,256]{4,1,3,2,0:T(8,128)} %copy-done.2, f32[3,16,8,32,256]{4,1,3,2,0:T(8,128)} %get-tuple-element.194, f32[8,32,256]{2,1,0:T(8,128)S(1)} %fusion.38), kind=kLoop, calls=%fused_computation.62 | loop fusion | flops 6291456 | bytes 38010880 | tf_op jit(solution)/shard_map/add | solution.py:114
  769.8 10.5 %slice_bitcast_fusion.1 = (f32[1,3,8,8,32,256]{5,2,4,3,1,0:T(8,128)}, f32[1,3,8,8,32,256]{5,2,4,3,1,0:T(8,128)}) fusion(f32[3,16,8,32,256]{4,1,3,2,0:T(8,128)} %multiply_add_fusion.2), kind=kLoop, calls=%fused_computation.65 | loop fusion | bytes 25165824 | tf_op jit(solution)/shard_map/stack | solution.py:116
  780.4 10.8 %pad_maximum_fusion.8 = f32[2,3,8,8,32,256]{5,2,4,3,1,0:T(8,128)} fusion(f32[1,3,8,8,32,256]{5,2,4,3,1,0:T(8,128)} %get-tuple-element.240, f32[1,3,8,8,32,256]{5,2,4,3,1,0:T(8,128)} %get-tuple-element.239), kind=kLoop, calls=%fused_computation.60 | loop fusion | flops 3145728 | bytes 25165824 | tf_op jit(solution)/shard_map/stack | solution.py:116
  791.2 120.1 %all_to_all.24 = f32[2,3,8,8,32,256]{5,2,4,3,1,0:T(8,128)} all-to-all(f32[2,3,8,8,32,256]{5,2,4,3,1,0:T(8,128)} %pad_maximum_fusion.8), channel_id=1, replica_groups=mesh['space'=16,'mode'=2] {'mode'}, dimensions={0} | all-to-all | bytes 25165824 | tf_op jit(solution)/shard_map/all_to_all | solution.py:116
  911.2 13.2 %copy.16 = f32[3,8,8,2,32,256]{5,4,3,2,1,0:T(8,128)} copy(f32[3,8,8,2,32,256]{5,1,4,2,0,3:T(8,128)} %bitcast.60) | data formatting | bytes 25165824 | tf_op jit(solution)/shard_map/reshape | solution.py:115
  (29 shorter events, 0.4 us)
Async XLA Ops:
  0.0 195.4 %copy-start = (s32[8,64,256]{2,1,0:T(8,128)S(1)}, s32[8,64,256]{2,1,0:T(8,128)}, u32[]{:S(2)}) copy-start(s32[8,64,256]{2,1,0:T(8,128)} %param.15) | copy-start | bytes 1572868
  182.4 11.9 %copy-start.9 = (f32[16,16,16,1]{2,1,3,0:T(8,128)S(1)}, f32[16,16,16,1]{2,1,3,0:T(8,128)}, u32[]{:S(2)}) copy-start(f32[16,16,16,1]{2,1,3,0:T(8,128)} %constant.101) | copy-start | bytes 49156
  182.4 11.9 %copy-start.10 = (f32[3,8,16]{2,1,0:T(8,128)S(1)}, f32[3,8,16]{2,1,0:T(8,128)}, u32[]{:S(2)}) copy-start(f32[3,8,16]{2,1,0:T(8,128)} %param.14) | copy-start | bytes 4612
  182.4 13.0 %copy-start.7 = (f32[8,64,256]{2,1,0:T(8,128)S(1)}, f32[8,64,256]{2,1,0:T(8,128)}, u32[]{:S(2)}) copy-start(f32[8,64,256]{2,1,0:T(8,128)} %param.12) | copy-start | bytes 1572868
  182.4 13.0 %copy-start.8 = (f32[8,64,256]{2,1,0:T(8,128)S(1)}, f32[8,64,256]{2,1,0:T(8,128)}, u32[]{:S(2)}) copy-start(f32[8,64,256]{2,1,0:T(8,128)} %param.13) | copy-start | bytes 1572868
  182.4 18.5 %copy-start.6 = (s32[8,64,256]{2,1,0:T(8,128)S(1)}, s32[8,64,256]{2,1,0:T(8,128)}, u32[]{:S(2)}) copy-start(s32[8,64,256]{2,1,0:T(8,128)} %param.16) | copy-start | bytes 1572868
  188.7 72.6 %collective-permute-start = (f32[3,16,2,32,256]{4,1,3,2,0:T(8,128)}, f32[3,16,2,32,256]{4,1,3,2,0:T(8,128)}, u32[]{:S(2)}, u32[]{:S(2)}) collective-permute-start(f32[3,16,2,32,256]{4,1,3,2,0:T(8,128)} %get-tuple-element.245), channel_id=1, source_target_pairs={{0,2},{2,4},{4,6},{6,8},{8,10},{10,12},{12,14},{14,16},{16,18},{18... | collective-permute-start | bytes 9437192 | tf_op jit(solution)/shard_map/ppermute | solution.py:19
  190.6 70.7 %collective-permute-start.1 = (f32[3,16,2,32,256]{4,1,3,2,0:T(8,128)}, f32[3,16,2,32,256]{4,1,3,2,0:T(8,128)}, u32[]{:S(2)}, u32[]{:S(2)}) collective-permute-start(f32[3,16,2,32,256]{4,1,3,2,0:T(8,128)} %get-tuple-element.246), channel_id=1, source_target_pairs={{2,0},{4,2},{6,4},{8,6},{10,8},{12,10},{14,12},{16,14},{18,16},{20... | collective-permute-start | bytes 9437192 | tf_op jit(solution)/shard_map/ppermute | solution.py:20
  196.7 10.7 %collective-permute-start.2 = (f32[3,16,8,1,256]{4,1,3,2,0:T(8,128)S(1)}, f32[3,16,8,1,256]{4,1,3,2,0:T(8,128)}, u32[]{:S(2)}, u32[]{:S(2)}) collective-permute-start(f32[3,16,8,1,256]{4,1,3,2,0:T(8,128)S(1)} %get-tuple-element.247), channel_id=1, source_target_pairs={{0,1},{2,3},{4,5},{6,7},{8,9},{10,11},{12,13},{14,15},{16,17},{18,... | collective-permute-start | bytes 1179656 | tf_op jit(solution)/shard_map/ppermute | solution.py:19
  199.7 12.7 %collective-permute-start.3 = (f32[3,16,8,1,256]{4,1,3,2,0:T(8,128)S(1)}, f32[3,16,8,1,256]{4,1,3,2,0:T(8,128)}, u32[]{:S(2)}, u32[]{:S(2)}) collective-permute-start(f32[3,16,8,1,256]{4,1,3,2,0:T(8,128)S(1)} %get-tuple-element.248), channel_id=1, source_target_pairs={{1,0},{3,2},{5,4},{7,6},{9,8},{11,10},{13,12},{15,14},{17,16},{19,... | collective-permute-start | bytes 1179656 | tf_op jit(solution)/shard_map/ppermute | solution.py:20
  476.5 6.6 copy-start.2
  477.3 72.3 %collective-permute-start.4 = (f32[3,16,2,32,256]{4,1,3,2,0:T(8,128)S(1)}, f32[3,16,2,32,256]{4,1,3,2,0:T(8,128)S(1)}, u32[]{:S(2)}, u32[]{:S(2)}) collective-permute-start(f32[3,16,2,32,256]{4,1,3,2,0:T(8,128)S(1)} %get-tuple-element.241), channel_id=1, source_target_pairs={{0,2},{2,4},{4,6},{6,8},{8,10},{10,12},{12,14},{14,16},{16,18},{18... | collective-permute-start | bytes 9437192 | tf_op jit(solution)/shard_map/ppermute | solution.py:19
  479.4 71.9 %collective-permute-start.5 = (f32[3,16,2,32,256]{4,1,3,2,0:T(8,128)S(1)}, f32[3,16,2,32,256]{4,1,3,2,0:T(8,128)}, u32[]{:S(2)}, u32[]{:S(2)}) collective-permute-start(f32[3,16,2,32,256]{4,1,3,2,0:T(8,128)S(1)} %get-tuple-element.242), channel_id=1, source_target_pairs={{2,0},{4,2},{6,4},{8,6},{10,8},{12,10},{14,12},{16,14},{18,16},{20... | collective-permute-start | bytes 9437192 | tf_op jit(solution)/shard_map/ppermute | solution.py:20
  483.1 9.5 %collective-permute-start.6 = (f32[3,16,8,1,256]{4,1,3,2,0:T(8,128)S(1)}, f32[3,16,8,1,256]{4,1,3,2,0:T(8,128)S(1)}, u32[]{:S(2)}, u32[]{:S(2)}) collective-permute-start(f32[3,16,8,1,256]{4,1,3,2,0:T(8,128)S(1)} %get-tuple-element.243), channel_id=1, source_target_pairs={{0,1},{2,3},{4,5},{6,7},{8,9},{10,11},{12,13},{14,15},{16,17},{18,... | collective-permute-start | bytes 1179656 | tf_op jit(solution)/shard_map/ppermute | solution.py:19
  485.4 11.4 %collective-permute-start.7 = (f32[3,16,8,1,256]{4,1,3,2,0:T(8,128)S(1)}, f32[3,16,8,1,256]{4,1,3,2,0:T(8,128)S(1)}, u32[]{:S(2)}, u32[]{:S(2)}) collective-permute-start(f32[3,16,8,1,256]{4,1,3,2,0:T(8,128)S(1)} %get-tuple-element.244), channel_id=1, source_target_pairs={{1,0},{3,2},{5,4},{7,6},{9,8},{11,10},{13,12},{15,14},{17,16},{19,... | collective-permute-start | bytes 1179656 | tf_op jit(solution)/shard_map/ppermute | solution.py:20
  492.7 56.9 %copy-start.4 = (f32[3,16,8,1,256]{4,1,3,2,0:T(8,128)}, f32[3,16,8,1,256]{4,1,3,2,0:T(8,128)S(1)}, u32[]{:S(2)}) copy-start(f32[3,16,8,1,256]{4,1,3,2,0:T(8,128)S(1)} %collective-permute-done.6) | copy-start | bytes 1179652
  496.8 52.8 %copy-start.5 = (f32[3,16,8,1,256]{4,1,3,2,0:T(8,128)}, f32[3,16,8,1,256]{4,1,3,2,0:T(8,128)S(1)}, u32[]{:S(2)}) copy-start(f32[3,16,8,1,256]{4,1,3,2,0:T(8,128)S(1)} %collective-permute-done.7) | copy-start | bytes 1179652
  549.6 1.7 copy-start.3
  911.2 13.2 %copy-start.1 = (s32[8,64,256]{2,1,0:T(8,128)S(1)}, s32[8,64,256]{2,1,0:T(8,128)}, u32[]{:S(2)}) copy-start(s32[8,64,256]{2,1,0:T(8,128)} %param.15) | copy-start | bytes 1572868
